TPU v7x, 128 devices: a whole 4x4x4 slice. The times are simulated.
128 devices in a mesh: req: 16 (over x, z), exp: 8 (over y, core).
Axes of the slice: x: 4, y: 4, z: 4, core: 2. Of those that a mesh axis runs over, the one named last changes fastest.
Arguments:
- tokens: bfloat16 [16384, 2048], P('req'), may hold values from -40 to 40
- routes: int32 [16384, 2], P('req'), may hold values from 0 to 7, all different within a row; in each aligned block of 1024 rows (0 to 1023, 1024 to 2047, ...) at most 320 rows name the same one
- lengths: int32 [64], P('req'), may hold values from 1 to 256, 8192 in all
- cached_prefix_length: int32 [64], P('req'), may hold values from 0 to 64, as said below
- prefix_cache_row: int32 [64], replicated, may hold values from 0 to 15, as said below
- adapter_per_request: int32 [64], P('req'), may hold values from 0 to 63
- adapter_storage_slot: int32 [64], replicated, may hold values from 0 to 63, each once
- router_weight: bfloat16 [2048, 8], replicated, may hold values from -0.125 to 0.125
- key_value_weight: bfloat16 [2048, 4096], P('req', 'exp'), may hold values from -0.125 to 0.125
- expert_query_weight: bfloat16 [2048, 8, 2048], P('req', None, 'exp'), may hold values from -0.125 to 0.125
- expert_output_weight: bfloat16 [8, 2048, 2048], P(None, 'exp', 'req'), may hold values from -0.125 to 0.125
- adapter_down_maps: bfloat16 [64, 2048, 16], P('req'), may hold values from -0.125 to 0.125
- adapter_up_maps: bfloat16 [64, 16, 4096], P('req', None, 'exp'), may hold values from -1.5 to 1.5
- prefix_cache_store: bfloat16 [64, 64, 4096], P('req', None, 'exp'), may hold values from -6 to 6
Outputs:
- attention_out: bfloat16 [16384, 2048], P('req', 'exp')
Inputs may be any that keep to these rules, and one draw needn't show every extreme that they name: `routes`: in each aligned block of 1024 rows (one group) no expert is named by more than 320 rows, and one is named by exactly 320. The lengths sum to 8192 and some request has exactly 256. `cached_prefix_length`: exactly 32 requests have no cached prefix; some request has exactly 64. `prefix_cache_row`: request j of a group keeps its cache in slot j of its row; each row holds exactly one cache in each slot, and no row holds two caches of one group. `adapter_storage_slot`: each slot holds one adapter.
All inputs are finite; a program needn't handle non-finite values. No bound on the sum of `lengths` on one device may be relied on, other than what follows from the above.
Results may differ from a plain program's by a relative error of at most 0.017.
The roundings to bfloat16 on the way count: a program that leaves them out, or rounds other values in their place, can miss the bound.
Values may be sent and summed in bfloat16 or wider, within the bound.
No kernel may reach another device: no remote copies, remote signals or barrier semaphores. Data moves between devices by JAX's collectives and lax.ppermute only.
A program may use at most 128 MiB of HBM per device.

v0:
```python
import jax
import jax.numpy as jnp
from jax import lax
from jax.sharding import PartitionSpec as P

HD = 128
NE = 8
TOPK = 2
CAP = 320
adapter_scale = 0.5


def compact(routes):
    route_flat = routes.reshape(-1)
    pair_count = route_flat.shape[0]
    one_hot = (route_flat[:, None] == jnp.arange(NE, dtype=jnp.int32)[None, :]).astype(jnp.int32)
    earlier = jnp.cumsum(one_hot, axis=0) - one_hot
    route_rank = jnp.sum(earlier * one_hot, axis=1)
    slot_table = (
        jnp.zeros((NE, CAP), jnp.int32)
        .at[route_flat, route_rank]
        .set(jnp.arange(pair_count, dtype=jnp.int32))
    )
    return (route_flat, route_rank, slot_table)


def attend(queries, all_keys, cached_prefix_length):
    per_request = queries.shape[1]
    key_span = all_keys.shape[1]
    cached = key_span - per_request
    scores = jnp.einsum(
        "rtjhd,rshd->rhtjs", queries, all_keys[:, :, :, 0, :], preferred_element_type=jnp.float32
    ) * queries.shape[-1] ** (-0.5)
    key_place = jnp.arange(key_span, dtype=jnp.int32)
    query_place = jnp.arange(per_request, dtype=jnp.int32)
    from_cache = key_place[None, :] < cached_prefix_length[:, None]
    from_prompt = (key_place[None, :] >= cached) & (
        key_place[None, :] - cached <= query_place[:, None]
    )
    allowed = jnp.where(
        key_place[None, None, :] < cached, from_cache[:, None, :], from_prompt[None, :, :]
    )
    allowed = allowed[:, None, :, None, :]
    row_max = jnp.max(jnp.where(allowed, scores, -jnp.inf), axis=-1, keepdims=True)
    weights = jnp.where(allowed, jnp.exp(scores - row_max), 0.0)
    probability = (weights / jnp.sum(weights, axis=-1, keepdims=True)).astype(jnp.bfloat16)
    return jnp.einsum(
        "rhtjs,rshd->rtjhd",
        probability,
        all_keys[:, :, :, 1, :],
        preferred_element_type=jnp.float32,
    ).astype(jnp.bfloat16)


def body(
    tokens,
    routes,
    lengths,
    cached_prefix_length,
    prefix_cache_row,
    adapter_per_request,
    adapter_storage_slot,
    router_weight,
    key_value_weight,
    expert_query_weight,
    expert_output_weight,
    adapter_down_maps,
    adapter_up_maps,
    prefix_cache_store,
):
    group_index = lax.axis_index("req")
    num_requests = lengths.shape[0]
    tok_rows = tokens.shape[0]
    per_request = tok_rows // num_requests
    model_width = tokens.shape[1]
    kv_cols = key_value_weight.shape[1]
    query_cols = expert_query_weight.shape[2]
    heads = kv_cols // (2 * HD)
    cached = prefix_cache_store.shape[1]
    route_flat, route_rank, slot_table = compact(routes)
    picked = tokens[slot_table // 2]
    pieces = (
        lax.all_gather(key_value_weight, "req", axis=0, tiled=True),
        lax.all_gather(expert_query_weight, "req", axis=0, tiled=True),
    )
    key_value_segment = jnp.dot(tokens, pieces[0], preferred_element_type=jnp.float32)
    query_run = jnp.einsum("kcd,dkh->kch", picked, pieces[1], preferred_element_type=jnp.float32)
    adapter_hot = (
        adapter_per_request[:, None]
        == jnp.arange(adapter_storage_slot.shape[0], dtype=jnp.int32)[None, :]
    ).astype(jnp.int32)
    wanted = jnp.sum(adapter_hot * adapter_storage_slot[None, :], axis=1)
    pieces = (
        lax.all_gather(adapter_down_maps, "req", axis=0, tiled=True),
        lax.all_gather(adapter_up_maps, "req", axis=0, tiled=True),
    )
    row_count = pieces[0].shape[0]
    matches = (wanted[:, None] == jnp.arange(row_count, dtype=jnp.int32)[None, :]).astype(
        jnp.bfloat16
    )
    down_run = jnp.einsum("rn,ndq->rdq", matches, pieces[0], preferred_element_type=jnp.float32)
    up_run = jnp.einsum("rn,nqc->rqc", matches, pieces[1], preferred_element_type=jnp.float32)
    reduced_rank_state = jnp.einsum(
        "rtd,rdq->rtq",
        tokens.reshape(num_requests, per_request, model_width),
        down_run.astype(jnp.bfloat16),
        preferred_element_type=jnp.float32,
    ).astype(jnp.bfloat16)
    adapter_term = jnp.einsum(
        "mdg,mgy->mdy",
        reduced_rank_state,
        up_run.astype(jnp.bfloat16),
        preferred_element_type=jnp.float32,
    ).reshape(tok_rows, kv_cols)
    fresh_key_value = (key_value_segment + adapter_scale * adapter_term).astype(jnp.bfloat16)
    own_rows = lax.dynamic_slice_in_dim(
        prefix_cache_row, group_index * num_requests, num_requests, 0
    )
    wanted_slot = own_rows * num_requests + jnp.arange(num_requests, dtype=jnp.int32)
    shard_piece = lax.all_gather(prefix_cache_store, "req", axis=0, tiled=True)
    row_count = shard_piece.shape[0]
    matches = (wanted_slot[:, None] == jnp.arange(row_count, dtype=jnp.int32)[None, :]).astype(
        jnp.bfloat16
    )
    stored = jnp.einsum(
        "rn,nsc->rsc", matches, shard_piece, preferred_element_type=jnp.float32
    ).astype(jnp.bfloat16)
    all_keys = jnp.concatenate(
        [stored, fresh_key_value.reshape(num_requests, per_request, kv_cols)], axis=1
    )
    all_keys = all_keys.reshape(num_requests, cached + per_request, heads, 2, HD)
    queries = query_run.astype(jnp.bfloat16)[route_flat, route_rank].reshape(
        num_requests, per_request, TOPK, heads, HD
    )
    attended = attend(queries, all_keys, cached_prefix_length)
    gathered = attended.reshape(TOPK * tok_rows, query_cols)[slot_table]
    logits = jnp.dot(tokens, router_weight, preferred_element_type=jnp.float32)
    route_hot = (routes[:, :, None] == jnp.arange(NE, dtype=jnp.int32)[None, None, :]).astype(
        jnp.float32
    )
    chosen = jnp.sum(route_hot * logits[:, None, :], axis=-1)
    gate_values = jax.nn.sigmoid(chosen - chosen[:, ::-1])
    live_rows = (
        (jnp.arange(per_request, dtype=jnp.int32)[None, :] < lengths[:, None])
        .reshape(tok_rows)
        .astype(jnp.float32)
    )
    shard_piece = lax.all_gather(expert_output_weight, "req", axis=2, tiled=True)
    out_blocks = jnp.einsum(
        "kch,khn->kcn", gathered, shard_piece, preferred_element_type=jnp.float32
    )
    per_pair = out_blocks[route_flat, route_rank].reshape(tok_rows, TOPK, shard_piece.shape[2])
    partial_value = jnp.sum(per_pair * gate_values[:, :, None], axis=1) * live_rows[:, None]
    return lax.psum_scatter(
        partial_value.astype(jnp.bfloat16), "exp", scatter_dimension=1, tiled=True
    )


def solution(mesh):
    return jax.shard_map(
        body,
        mesh=mesh,
        in_specs=(
            P("req", None),
            P("req", None),
            P("req"),
            P("req"),
            P(),
            P("req"),
            P(),
            P(),
            P("req", "exp"),
            P("req", None, "exp"),
            P(None, "exp", "req"),
            P("req", None, None),
            P("req", None, "exp"),
            P("req", None, "exp"),
        ),
        out_specs=P("req", "exp"),
        check_vma=False,
    )
```

profile of v0, /device:TPU:0, one launch (start us, length us, event | category | flops | bytes accessed | tf_op | source)
XLA Modules:
  0.0 522.8 jit_solution(609906091671764247)
XLA Ops:
  6.5 0.7 all-gather.13.cloned.1.call-update
  7.3 0.0 all-gather.7.cloned.1.call-start
  7.3 0.7 all-gather.7.cloned.1.call-update
  8.0 0.0 all-gather.11.cloned.1.call-start
  8.1 0.7 all-gather.11.cloned.1.call-update
  8.8 0.5 all-gather.9.cloned.1.call-update
  9.3 0.0 all-gather.15.cloned.1.call-start
  9.4 1.9 copy.58
  11.3 0.0 all-gather.17.cloned.1.call-start
  11.4 0.5 all-gather.17.cloned.1.call-update
  11.9 0.0 reduce-scatter.2.cloned.1.call-start
  12.0 0.9 copy.55
  12.9 0.3 eq.90
  13.2 0.3 eq.86
  13.4 0.3 reshape.176
  13.8 2.3 reduce-window.6
  16.0 0.3 slice_reduce_fusion
  16.3 0.2 reduce-window.9
  16.5 0.1 add_bitcast_fusion
  16.7 0.1 multiply_reduce_fusion.1
  16.8 0.1 and_reduce_fusion
  16.9 8.1 %scatter_custom_fusion = s32[2560]{0:T(1024)S(1)} fusion(s32[2048]{0:T(1024)S(1)} %broadcast_select_fusion.1, s32[2048]{0:T(1024)S(1)} %iota.56, s32[]{:T(128)} %constant.20.clone.1), kind=kCustom, calls=%fused_computation.75 | custom fusion | bytes 10244
  25.0 0.1 reshape.184
  25.1 0.1 reshape.188
  25.2 0.1 reshape.202
  25.3 22.9 %gather_fusion = bf16[2560,2048]{1,0:T(8,128)(2,1)} fusion(bf16[1024,2048]{1,0:T(8,128)(2,1)} %param.14, s32[3072]{0:T(1024)S(1)} %pad_clamp_fusion.1), kind=kCustom, calls=%fused_computation | custom fusion | bytes 20981760 | tf_op jit(solution)/shard_map/gather | solution.py:81
  48.2 3.4 fusion.60
  51.7 0.4 rev.3
  52.1 0.2 copy.61
  52.3 0.1 convert_bitcast_fusion
  52.4 0.1 iota_add_fusion.1
  52.6 0.2 select_reduce_fusion.2
  52.7 0.1 iota_compare_fusion.4
  52.8 0.2 fusion.32
  53.0 0.3 broadcast_select_fusion
  53.3 1.6 all-gather.13.cloned.1.call-done
  54.8 3.0 convolution_convert_fusion.1
  57.9 50.1 %all-gather.7.cloned.1.call-done = bf16[64,64,512]{2,1,0:T(8,128)(2,1)} async-done(((bf16[4,64,512]{2,1,0:T(8,128)(2,1)}), bf16[64,64,512]{2,1,0:T(8,128)(2,1)}) %all-gather.7.cloned.1.call-update) | async-done | bytes 4194320 | tf_op jit(solution)/shard_map/all_gather | solution.py:120
  107.9 6.7 %fusion.21 = bf16[4,64,512]{2,0,1:T(4,128)(2,1)S(1)} fusion(bf16[64,64,512]{2,1,0:T(8,128)(2,1)} %all-gather.7.cloned.1.call-done, s32[4]{0:T(128)S(1)} %iota_add_fusion.1), kind=kOutput, calls=%fused_computation.29 | convolution fusion | flops 16908544 | bytes 4456464 | tf_op jit(solution)/shard_map/rn,nsc->rsc/dot_general | solution.py:125
  114.6 0.1 concatenate.13
  114.8 46.6 %all-gather.11.cloned.1.call-done = bf16[64,2048,16]{1,2,0:T(8,128)(2,1)} async-done(((bf16[4,2048,16]{1,2,0:T(8,128)(2,1)}), bf16[64,2048,16]{1,2,0:T(8,128)(2,1)}) %all-gather.11.cloned.1.call-update) | async-done | bytes 4194320 | tf_op jit(solution)/shard_map/all_gather | solution.py:94
  161.4 6.7 %fusion.15 = bf16[4,2048,16]{1,0,2:T(4,128)(2,1)S(1)} fusion(bf16[64,2048,16]{1,2,0:T(8,128)(2,1)} %all-gather.11.cloned.1.call-done, s32[4]{0:T(128)S(1)} %select_reduce_fusion.2), kind=kOutput, calls=%fused_computation.22 | convolution fusion | flops 16908544 | bytes 4456464 | tf_op jit(solution)/shard_map/rn,ndq->rdq/dot_general | solution.py:101
  168.1 4.0 convolution_multiply_fusion
  172.0 36.2 %all-gather.9.cloned.1.call-done = bf16[2048,512]{1,0:T(8,128)(2,1)} async-done(((bf16[128,512]{1,0:T(8,128)(2,1)}), bf16[2048,512]{1,0:T(8,128)(2,1)}) %all-gather.9.cloned.1.call-update) | async-done | bytes 2097168 | tf_op jit(solution)/shard_map/all_gather | solution.py:83
  208.2 6.2 %fusion.18 = bf16[1024,512]{1,0:T(8,128)(2,1)} fusion(f32[4,256,512]{2,1,0:T(8,128)S(1)} %convolution_multiply_fusion, bf16[1024,2048]{1,0:T(8,128)(2,1)} %param.14, bf16[2048,512]{1,0:T(8,128)(2,1)} %all-gather.9.cloned.1.call-done), kind=kOutput, calls=%fused_computation.24 | convolution fusion | flops 2148532224 | bytes 9437184 | tf_op jit(solution)/shard_map/dot_general | solution.py:86
  214.5 1.3 concatenate.14
  215.8 0.1 copy_dynamic-update-slice_fusion.1
  215.9 0.3 copy_dynamic-update-slice_fusion
  216.2 64.2 %all-gather.15.cloned.1.call-done = bf16[2048,8,256]{2,0,1:T(8,128)(2,1)} async-done(((bf16[128,8,256]{2,0,1:T(8,128)(2,1)}), bf16[2048,8,256]{2,0,1:T(8,128)(2,1)}) %all-gather.15.cloned.1.call-update) | async-done | bytes 8388624 | tf_op jit(solution)/shard_map/all_gather | solution.py:84
  280.4 9.2 %convolution_convert_fusion = bf16[8,320,256]{2,1,0:T(8,128)(2,1)S(1)} fusion(bf16[8,320,2048]{2,1,0:T(8,128)(2,1)} %bitcast.79, bf16[2048,8,256]{2,0,1:T(8,128)(2,1)} %all-gather.15.cloned.1.call-done), kind=kOutput, calls=%fused_computation.26 | convolution fusion | flops 2685009920 | bytes 20185088 | tf_op jit(solution)/shard_map/kcd,dkh->kch/dot_general | solution.py:87
  289.7 11.1 %gather_fusion.1 = bf16[2048,256]{1,0:T(8,128)(2,1)S(1)} fusion(bf16[8,320,256]{2,1,0:T(8,128)(2,1)S(1)} %convolution_convert_fusion, s32[2048]{0:T(1024)S(1)} %bitcast.76), kind=kCustom, calls=%fused_computation.1 | custom fusion | bytes 2113536 | tf_op jit(solution)/shard_map/gather | solution.py:132
  300.8 0.3 reshape.178
  301.1 6.3 %fusion.54 = (f32[4,2,256,2]{2,3,1,0:T(2,128)S(1)}, f32[4,2,256,2,320]{2,4,3,1,0:T(8,128)}) fusion(pred[4,256,320]{1,2,0:T(8,128)(4,1)S(1)} %broadcast_select_fusion, bf16[4,256,2,2,128]{4,3,2,1,0:T(2,128)(2,1)S(1)} %reshape.178, bf16[4,320,2,2,128]{4,1,2,0,3:T(8,128)(2,1)} %copy-done.2), kind=kOutput, calls=%fused_computation.96 | convolution fusion | flops 678953280 | bytes 9322496 | tf_op jit(solution)/shard_map/sub | solution.py:45
  307.4 3.3 fusion.20
  310.6 0.8 copy.60
  311.4 0.1 copy.98
  311.6 7.6 %gather_fusion.2 = bf16[2560,256]{1,0:T(8,128)(2,1)S(1)} fusion(bf16[2048,256]{1,0:T(8,128)(2,1)S(1)} %bitcast.78, s32[3072]{0:T(1024)S(1)} %pad_clamp_fusion), kind=kCustom, calls=%fused_computation.2 | custom fusion | bytes 2631680 | tf_op jit(solution)/shard_map/gather | solution.py:136
  319.2 41.3 %all-gather.17.cloned.1.call-done = bf16[8,256,2048]{2,1,0:T(8,128)(2,1)} async-done(((bf16[8,256,128]{2,1,0:T(8,128)(2,1)}), bf16[8,256,2048]{2,1,0:T(8,128)(2,1)}) %all-gather.17.cloned.1.call-update) | async-done | bytes 8388624 | tf_op jit(solution)/shard_map/all_gather | solution.py:148
  360.5 12.0 %fusion.59 = f32[8,320,2048]{2,1,0:T(8,128)} fusion(bf16[8,320,256]{2,1,0:T(8,128)(2,1)S(1)} %bitcast.80, bf16[8,256,2048]{2,1,0:T(8,128)(2,1)} %all-gather.17.cloned.1.call-done), kind=kOutput, calls=%fused_computation.97 | convolution fusion | flops 2684354560 | bytes 30670848 | tf_op jit(solution)/shard_map/kch,khn->kcn/dot_general | solution.py:149
  372.5 51.1 %gather_fusion.3 = f32[2048,2048]{1,0:T(8,128)} fusion(f32[8,320,2048]{2,1,0:T(8,128)} %fusion.59, s32[2048]{0:T(1024)S(1)} %bitcast.77), kind=kCustom, calls=%fused_computation.3 | custom fusion | bytes 33570816 | tf_op jit(solution)/shard_map/gather | solution.py:152
  423.6 20.0 %reshape.180 = f32[1024,2,2048]{2,1,0:T(2,128)} reshape(f32[2048,2048]{1,0:T(8,128)} %gather_fusion.3) | data formatting | bytes 33554432 | tf_op jit(solution)/shard_map/reshape | solution.py:152
  443.6 29.1 %multiply_reduce_fusion = f32[1024,2048]{1,0:T(8,128)} fusion(f32[1024,2,2048]{2,1,0:T(2,128)} %reshape.180, f32[1024,2]{1,0:T(8,128)S(1)} %copy.61), kind=kLoop, calls=%fused_computation.6 | loop fusion | flops 6291456 | bytes 25174016 | tf_op jit(solution)/shard_map/reduce_sum | solution.py:153
  472.8 5.8 %multiply_convert_fusion = bf16[1024,2048]{1,0:T(8,128)(2,1)} fusion(f32[1024,2048]{1,0:T(8,128)} %multiply_reduce_fusion, f32[1024]{0:T(1024)S(1)} %bitcast.83), kind=kLoop, calls=%fused_computation.7 | loop fusion | flops 4194304 | bytes 12587008 | tf_op jit(solution)/shard_map/convert_element_type | solution.py:155
  478.6 37.3 %reduce-scatter.2.cloned.1.call-done = bf16[1024,256]{1,0:T(8,128)(2,1)} async-done(((bf16[1024,2048]{1,0:T(8,128)(2,1)}), bf16[1024,256]{1,0:T(8,128)(2,1)}) %reduce-scatter.2.cloned.1.call-update) | async-done | bytes 524304 | tf_op jit(solution)/shard_map/reduce_scatter | solution.py:154
  (42 shorter events, 0.3 us)
Async XLA Ops:
  6.5 41.6 %copy-start = (bf16[2048,8]{0,1:T(8,128)(2,1)S(1)}, bf16[2048,8]{0,1:T(8,128)(2,1)}, u32[]{:S(2)}) copy-start(bf16[2048,8]{0,1:T(8,128)(2,1)} %param.21) | copy-start | bytes 98308
  6.5 10.2 %copy-start.7 = (s32[2]{0:T(128)S(1)}, s32[2]{0:T(128)}, u32[]{:S(2)}) copy-start(s32[2]{0:T(128)} %constant.62) | copy-start | bytes 28
  6.5 10.3 %copy-start.6 = (s32[2]{0:T(128)S(1)}, s32[2]{0:T(128)}, u32[]{:S(2)}) copy-start(s32[2]{0:T(128)} %constant.65) | copy-start | bytes 28
  6.5 48.3 %all-gather.13.cloned.1.call-start = ((), (), s32[]{:S(2)}) async-start(), calls=%async_computation.4 | async-start | bytes 1114112 | tf_op jit(solution)/shard_map/all_gather | solution.py:95
  7.3 100.7 %all-gather.7.cloned.1.call-start = ((), (), s32[]{:S(2)}) async-start(), calls=%async_computation.1 | async-start | bytes 4456448 | tf_op jit(solution)/shard_map/all_gather | solution.py:120
  8.0 153.3 %all-gather.11.cloned.1.call-start = ((), (), s32[]{:S(2)}) async-start(), calls=%async_computation.3 | async-start | bytes 4456448 | tf_op jit(solution)/shard_map/all_gather | solution.py:94
  8.7 199.5 %all-gather.9.cloned.1.call-start = ((), (), s32[]{:S(2)}) async-start(), calls=%async_computation.2 | async-start | bytes 2228224 | tf_op jit(solution)/shard_map/all_gather | solution.py:83
  9.3 271.1 %all-gather.15.cloned.1.call-start = ((), (), s32[]{:S(2)}) async-start(), calls=%async_computation.5 | async-start | bytes 8912896 | tf_op jit(solution)/shard_map/all_gather | solution.py:84
  11.3 349.2 %all-gather.17.cloned.1.call-start = ((), (), s32[]{:S(2)}) async-start(), calls=%async_computation.6 | async-start | bytes 8912896 | tf_op jit(solution)/shard_map/all_gather | solution.py:148
  11.9 504.0 %reduce-scatter.2.cloned.1.call-start = ((), (), s32[]{:S(2)}) async-start(), calls=%async_computation.7 | async-start | bytes 4718592 | tf_op jit(solution)/shard_map/reduce_scatter | solution.py:154
  48.1 3.5 copy-start.4
  48.1 4.2 copy-start.5
  48.1 4.3 copy-start.9
  48.2 4.4 copy-start.10
  48.2 4.4 copy-start.11
  48.2 4.6 copy-start.8
  216.2 64.2 %copy-start.2 = (bf16[4,320,2,2,128]{4,1,2,0,3:T(8,128)(2,1)}, bf16[4,320,2,2,128]{4,1,2,0,3:T(8,128)(2,1)S(1)}, u32[]{:S(2)}) copy-start(bf16[4,320,2,2,128]{4,1,2,0,3:T(8,128)(2,1)S(1)} %copy_dynamic-update-slice_fusion) | copy-start | bytes 3932164
  301.1 6.3 %copy-start.3 = (bf16[4,320,2,2,128]{4,1,2,0,3:T(8,128)(2,1)S(1)}, bf16[4,320,2,2,128]{4,1,2,0,3:T(8,128)(2,1)}, u32[]{:S(2)}) copy-start(bf16[4,320,2,2,128]{4,1,2,0,3:T(8,128)(2,1)} %copy-done.2) | copy-start | bytes 3932164
  472.8 43.2 %copy-start.1 = (bf16[2048,8]{0,1:T(8,128)(2,1)S(1)}, bf16[2048,8]{0,1:T(8,128)(2,1)}, u32[]{:S(2)}) copy-start(bf16[2048,8]{0,1:T(8,128)(2,1)} %param.21) | copy-start | bytes 98308
Sparse Core Ops, SparseCore 0:
  9.5 45.2 all-gather.12
  57.0 50.9 all-gather.6
  110.1 51.2 all-gather.10
  163.4 44.8 all-gather.8
  210.3 70.1 all-gather.14
  282.4 78.0 all-gather.16
  478.7 37.1 reduce-scatter.1
where the time goes:
time: 525 us; the launch traced here: 523 us
  waiting for transfers between devices  280 us (53%)
  local copies, waits for them, and re-layouts  129 us (25%)
  matrix products  60.9 us (12%)
  other arithmetic  38.7 us (7%)
  between operations  13.8 us (3%)
    all_gather x1, waiting for transfers between devices, body(): lax.all_gather(expert_query_weight, 'req', axis=0, tiled=True)  64.2 us
    gather x1, local copies, waits for them, and re-layouts, body(): out_blocks[route_flat, route_rank]  51.1 us
    all_gather x1, waiting for transfers between devices, body(): shard_piece = lax.all_gather(prefix_cache_store, 'req', axis=0, tiled=True)  50.1 us
    all_gather x1, waiting for transfers between devices, body(): lax.all_gather(adapter_down_maps, 'req', axis=0, tiled=True)  46.6 us
    all_gather x1, waiting for transfers between devices, body(): lax.all_gather(expert_output_weight, 'req', axis=2, tiled=True)  41.3 us
    reduce_scatter x1, waiting for transfers between devices, body(): lax.psum_scatter(partial_value.astype(jnp.bfloat16), 'exp', scatter_dimen...  37.3 us
    all_gather x1, waiting for transfers between devices, body(): lax.all_gather(key_value_weight, 'req', axis=0, tiled=True)  36.2 us
    reduce_sum x1, other arithmetic, body(): jnp.sum(per_pair * gate_values[:, :, None], axis=1) * live_rows[:, None]  29.1 us
  transfers between devices with their start and end apart: 7, of which 7 were waited for; matrix products, arithmetic and copies ran while one was open for 21% of the time, Pallas kernels for 0%

commit v1 on v0

--- a/solution.py
+++ b/solution.py
@@ -8,6 +8,13 @@
 TOPK = 2
 CAP = 320
 adapter_scale = 0.5
+
+
+def exchange_gather(shard, mesh_axis, dim):
+    peers = lax.axis_size(mesh_axis)
+    shards = jnp.stack([shard for _ in range(peers)])
+    shards = lax.all_to_all(shards, mesh_axis, split_axis=0, concat_axis=0)
+    return jnp.concatenate(shards, axis=dim)
 
 
 def compact(routes):
@@ -81,7 +88,7 @@
     picked = tokens[slot_table // 2]
     pieces = (
         lax.all_gather(key_value_weight, "req", axis=0, tiled=True),
-        lax.all_gather(expert_query_weight, "req", axis=0, tiled=True),
+        exchange_gather(expert_query_weight, "req", 0),
     )
     key_value_segment = jnp.dot(tokens, pieces[0], preferred_element_type=jnp.float32)
     query_run = jnp.einsum("kcd,dkh->kch", picked, pieces[1], preferred_element_type=jnp.float32)

time: 525 us -> 559 us (1.065)
  local copies, waits for them, and re-layouts: 129 us -> 142 us
  waiting for transfers between devices: 280 us -> 290 us
  starting transfers between devices: 0.23 us -> 8.34 us
    all_gather x1, waiting for transfers between devices: 1.58 us -> 90.6 us  [body(): lax.all_gather(adapter_up_maps, 'req', axis=0, tiled=True)]
    all_gather x1 -> x0, waiting for transfers between devices: 64.2 us -> none  [body(): lax.all_gather(expert_query_weight, 'req', axis=0, tiled=True)]
    all_gather x1, waiting for transfers between devices: 50.1 us -> 11.3 us  [body(): shard_piece = lax.all_gather(prefix_cache_store, 'req', axis=0, tiled=True)]
    all_to_all x0 -> x1, waiting for transfers between devices: none -> 12.6 us  [exchange_gather(): shards = lax.all_to_all(shards, mesh_axis, split_axis=0, concat_axis=0)]
    all_gather x1, waiting for transfers between devices: 41.3 us -> 51.6 us  [body(): lax.all_gather(expert_output_weight, 'req', axis=2, tiled=True)]
    all_to_all x0 -> x1, starting transfers between devices: none -> 8.14 us  [exchange_gather(): shards = lax.all_to_all(shards, mesh_axis, split_axis=0, concat_axis=0)]
    all_to_all x0 -> x1, local copies, waits for them, and re-layouts: none -> 7.83 us  [exchange_gather(): shards = lax.all_to_all(shards, mesh_axis, split_axis=0, concat_axis=0)]
    unnamed x30 -> x28, local copies, waits for them, and re-layouts: 11.2 us -> 10.9 us
  transfers between devices with their start and end apart: 7 -> 7, of which waited for: 7 -> 7; matrix products, arithmetic and copies ran while one was open for 21% -> 22% of each run, Pallas kernels for 0% -> 0%
where the time goes in v1:
time: 559 us; the launch traced here: 554 us
  waiting for transfers between devices  290 us (52%)
  local copies, waits for them, and re-layouts  142 us (25%)
  matrix products  61.1 us (11%)
  other arithmetic  38.7 us (7%)
  between operations  14 us (3%)
  starting transfers between devices  8.34 us (1%)
    all_gather x1, waiting for transfers between devices, body(): lax.all_gather(adapter_up_maps, 'req', axis=0, tiled=True)  90.6 us
    all_gather x1, waiting for transfers between devices, body(): lax.all_gather(expert_output_weight, 'req', axis=2, tiled=True)  51.6 us
    gather x1, local copies, waits for them, and re-layouts, body(): out_blocks[route_flat, route_rank]  51.1 us
    all_gather x1, waiting for transfers between devices, body(): lax.all_gather(adapter_down_maps, 'req', axis=0, tiled=True)  46.6 us
    reduce_scatter x1, waiting for transfers between devices, body(): lax.psum_scatter(partial_value.astype(jnp.bfloat16), 'exp', scatter_dimen...  37.3 us
    all_gather x1, waiting for transfers between devices, body(): lax.all_gather(key_value_weight, 'req', axis=0, tiled=True)  36.4 us
    reduce_sum x1, other arithmetic, body(): jnp.sum(per_pair * gate_values[:, :, None], axis=1) * live_rows[:, None]  29.1 us
    gather x1, local copies, waits for them, and re-layouts, body(): picked = tokens[slot_table // 2]  22.9 us
  transfers between devices with their start and end apart: 7, of which 7 were waited for; matrix products, arithmetic and copies ran while one was open for 22% of the time, Pallas kernels for 0%

profile of v1, /device:TPU:0, one launch (start us, length us, event | category | flops | bytes accessed | tf_op | source)
XLA Modules:
  0.0 554.1 jit_solution(10585575856939187122)
XLA Ops:
  6.5 0.7 all-gather.12.cloned.1.call-update
  7.3 0.0 all-gather.6.cloned.1.call-start
  7.3 0.7 all-gather.6.cloned.1.call-update
  8.1 0.7 all-gather.10.cloned.1.call-update
  8.8 0.5 all-gather.8.cloned.1.call-update
  9.4 0.5 all-gather.14.cloned.1.call-update
  9.9 1.1 copy.59
  11.1 4.4 stack.2
  15.4 8.1 %all-to-all-start = ((bf16[16,128,8,256]{3,1,2,0:T(8,128)(2,1)}), bf16[16,128,8,256]{3,1,2,0:T(8,128)(2,1)}, u32[]{:S(2)}, u32[]{:S(2)}) async-start(bf16[16,128,8,256]{3,1,2,0:T(8,128)(2,1)} %stack.2), calls=%async_computation | async-start | bytes 16777216 | tf_op jit(solution)/shard_map/all_to_all | solution.py:16
  23.6 0.0 reduce-scatter.2.cloned.1.call-start
  23.7 0.2 copy.56
  23.9 0.3 eq.90
  24.2 0.3 eq.86
  24.4 0.3 reshape.181
  24.8 2.3 reduce-window.6
  27.0 0.3 slice_reduce_fusion
  27.3 0.2 reduce-window.9
  27.5 0.1 add_bitcast_fusion
  27.7 0.1 multiply_reduce_fusion.1
  27.8 0.1 and_reduce_fusion
  27.9 8.5 %scatter_custom_fusion = s32[2560]{0:T(1024)S(1)} fusion(s32[2048]{0:T(1024)S(1)} %broadcast_select_fusion.1, s32[2048]{0:T(1024)S(1)} %iota.56, s32[]{:T(128)} %constant.20.clone.1), kind=kCustom, calls=%fused_computation.75 | custom fusion | bytes 10244
  36.5 0.1 reshape.190
  36.6 0.1 reshape.194
  36.6 0.1 reshape.208
  36.7 22.9 %gather_fusion = bf16[2560,2048]{1,0:T(8,128)(2,1)} fusion(bf16[1024,2048]{1,0:T(8,128)(2,1)} %param.14, s32[3072]{0:T(1024)S(1)} %pad_clamp_fusion.1), kind=kCustom, calls=%fused_computation | custom fusion | bytes 20981760 | tf_op jit(solution)/shard_map/gather | solution.py:88
  59.6 3.4 fusion.60
  63.1 0.2 rev.3
  63.4 0.2 copy.63
  63.6 0.1 convert_bitcast_fusion
  63.7 0.1 iota_add_fusion.1
  63.8 0.2 select_reduce_fusion.2
  64.0 0.1 iota_compare_fusion.4
  64.1 0.2 fusion.32
  64.2 0.3 broadcast_select_fusion
  64.5 90.6 %all-gather.12.cloned.1.call-done = bf16[64,16,512]{2,1,0:T(8,128)(2,1)} async-done(((bf16[4,16,512]{2,1,0:T(8,128)(2,1)}), bf16[64,16,512]{2,1,0:T(8,128)(2,1)}) %all-gather.12.cloned.1.call-update) | async-done | bytes 1048592 | tf_op jit(solution)/shard_map/all_gather | solution.py:102
  155.1 3.1 convolution_convert_fusion.1
  158.2 12.6 %all-to-all-done = bf16[16,128,8,256]{3,1,2,0:T(8,128)(2,1)} async-done(((bf16[16,128,8,256]{3,1,2,0:T(8,128)(2,1)}), bf16[16,128,8,256]{3,1,2,0:T(8,128)(2,1)}, u32[]{:S(2)}, u32[]{:S(2)}) %all-to-all-start) | async-done | bytes 8388640 | tf_op jit(solution)/shard_map/all_to_all | solution.py:16
  170.7 7.8 %copy.60 = bf16[16,128,8,256]{3,1,0,2:T(8,128)(2,1)} copy(bf16[16,128,8,256]{3,1,2,0:T(8,128)(2,1)} %all-to-all-done) | data formatting | bytes 16777216 | tf_op jit(solution)/shard_map/all_to_all | solution.py:16
  178.6 9.3 %convolution_convert_fusion = bf16[8,320,256]{2,1,0:T(8,128)(2,1)S(1)} fusion(bf16[8,320,2048]{2,1,0:T(8,128)(2,1)} %bitcast.80, bf16[2048,8,256]{2,0,1:T(8,128)(2,1)} %bitcast.81), kind=kOutput, calls=%fused_computation.26 | convolution fusion | flops 2685009920 | bytes 20185088 | tf_op jit(solution)/shard_map/kcd,dkh->kch/dot_general | solution.py:94
  187.8 11.1 %gather_fusion.1 = bf16[2048,256]{1,0:T(8,128)(2,1)S(1)} fusion(bf16[8,320,256]{2,1,0:T(8,128)(2,1)S(1)} %convolution_convert_fusion, s32[2048]{0:T(1024)S(1)} %bitcast.77), kind=kCustom, calls=%fused_computation.1 | custom fusion | bytes 2113536 | tf_op jit(solution)/shard_map/gather | solution.py:139
  199.0 1.3 reshape.184
  200.2 11.3 %all-gather.6.cloned.1.call-done = bf16[64,64,512]{2,1,0:T(8,128)(2,1)} async-done(((bf16[4,64,512]{2,1,0:T(8,128)(2,1)}), bf16[64,64,512]{2,1,0:T(8,128)(2,1)}) %all-gather.6.cloned.1.call-update) | async-done | bytes 4194320 | tf_op jit(solution)/shard_map/all_gather | solution.py:127
  211.6 6.7 %fusion.21 = bf16[4,64,512]{2,0,1:T(4,128)(2,1)S(1)} fusion(bf16[64,64,512]{2,1,0:T(8,128)(2,1)} %all-gather.6.cloned.1.call-done, s32[4]{0:T(128)S(1)} %iota_add_fusion.1), kind=kOutput, calls=%fused_computation.29 | convolution fusion | flops 16908544 | bytes 4456464 | tf_op jit(solution)/shard_map/rn,nsc->rsc/dot_general | solution.py:132
  218.3 0.1 concatenate.13
  218.4 46.6 %all-gather.10.cloned.1.call-done = bf16[64,2048,16]{1,2,0:T(8,128)(2,1)} async-done(((bf16[4,2048,16]{1,2,0:T(8,128)(2,1)}), bf16[64,2048,16]{1,2,0:T(8,128)(2,1)}) %all-gather.10.cloned.1.call-update) | async-done | bytes 4194320 | tf_op jit(solution)/shard_map/all_gather | solution.py:101
  265.0 6.7 %fusion.15 = bf16[4,2048,16]{1,0,2:T(4,128)(2,1)S(1)} fusion(bf16[64,2048,16]{1,2,0:T(8,128)(2,1)} %all-gather.10.cloned.1.call-done, s32[4]{0:T(128)S(1)} %select_reduce_fusion.2), kind=kOutput, calls=%fused_computation.22 | convolution fusion | flops 16908544 | bytes 4456464 | tf_op jit(solution)/shard_map/rn,ndq->rdq/dot_general | solution.py:108
  271.7 3.8 convolution_multiply_fusion
  275.5 36.4 %all-gather.8.cloned.1.call-done = bf16[2048,512]{1,0:T(8,128)(2,1)} async-done(((bf16[128,512]{1,0:T(8,128)(2,1)}), bf16[2048,512]{1,0:T(8,128)(2,1)}) %all-gather.8.cloned.1.call-update) | async-done | bytes 2097168 | tf_op jit(solution)/shard_map/all_gather | solution.py:90
  311.8 6.4 %fusion.18 = bf16[1024,512]{1,0:T(8,128)(2,1)} fusion(f32[4,256,512]{2,1,0:T(8,128)S(1)} %convolution_multiply_fusion, bf16[1024,2048]{1,0:T(8,128)(2,1)} %param.14, bf16[2048,512]{1,0:T(8,128)(2,1)} %all-gather.8.cloned.1.call-done), kind=kOutput, calls=%fused_computation.24 | convolution fusion | flops 2148532224 | bytes 9437184 | tf_op jit(solution)/shard_map/dot_general | solution.py:93
  318.3 1.4 concatenate.14
  319.7 0.8 copy_dynamic-update-slice_fusion.1
  320.5 1.2 copy_dynamic-update-slice_fusion
  321.7 6.3 %fusion.54 = (f32[4,2,256,2]{2,3,1,0:T(2,128)S(1)}, f32[4,2,256,2,320]{2,4,3,1,0:T(8,128)}) fusion(pred[4,256,320]{1,2,0:T(8,128)(4,1)S(1)} %broadcast_select_fusion, bf16[4,256,2,2,128]{4,3,2,1,0:T(2,128)(2,1)S(1)} %copy-done.2, bf16[4,320,2,2,128]{4,1,2,0,3:T(8,128)(2,1)} %copy_dynamic-update-slice_fusion), kind=kOutput, calls=%fused_computation.96 | convolution fusion | flops 678953280 | bytes 9322496 | tf_op jit(solution)/shard_map/sub | solution.py:52
  328.0 3.5 fusion.20
  331.5 0.8 copy.62
  332.3 0.1 copy.100
  332.4 7.6 %gather_fusion.2 = bf16[2560,256]{1,0:T(8,128)(2,1)S(1)} fusion(bf16[2048,256]{1,0:T(8,128)(2,1)S(1)} %bitcast.79, s32[3072]{0:T(1024)S(1)} %pad_clamp_fusion), kind=kCustom, calls=%fused_computation.2 | custom fusion | bytes 2631680 | tf_op jit(solution)/shard_map/gather | solution.py:143
  340.0 51.6 %all-gather.14.cloned.1.call-done = bf16[8,256,2048]{2,1,0:T(8,128)(2,1)} async-done(((bf16[8,256,128]{2,1,0:T(8,128)(2,1)}), bf16[8,256,2048]{2,1,0:T(8,128)(2,1)}) %all-gather.14.cloned.1.call-update) | async-done | bytes 8388624 | tf_op jit(solution)/shard_map/all_gather | solution.py:155
  391.6 12.0 %fusion.59 = f32[8,320,2048]{2,1,0:T(8,128)} fusion(bf16[8,320,256]{2,1,0:T(8,128)(2,1)S(1)} %bitcast.82, bf16[8,256,2048]{2,1,0:T(8,128)(2,1)} %all-gather.14.cloned.1.call-done), kind=kOutput, calls=%fused_computation.97 | convolution fusion | flops 2684354560 | bytes 30670848 | tf_op jit(solution)/shard_map/kch,khn->kcn/dot_general | solution.py:156
  403.6 51.1 %gather_fusion.3 = f32[2048,2048]{1,0:T(8,128)} fusion(f32[8,320,2048]{2,1,0:T(8,128)} %fusion.59, s32[2048]{0:T(1024)S(1)} %bitcast.78), kind=kCustom, calls=%fused_computation.3 | custom fusion | bytes 33570816 | tf_op jit(solution)/shard_map/gather | solution.py:159
  454.7 20.0 %reshape.186 = f32[1024,2,2048]{2,1,0:T(2,128)} reshape(f32[2048,2048]{1,0:T(8,128)} %gather_fusion.3) | data formatting | bytes 33554432 | tf_op jit(solution)/shard_map/reshape | solution.py:159
  474.7 29.1 %multiply_reduce_fusion = f32[1024,2048]{1,0:T(8,128)} fusion(f32[1024,2,2048]{2,1,0:T(2,128)} %reshape.186, f32[1024,2]{1,0:T(8,128)S(1)} %copy.63), kind=kLoop, calls=%fused_computation.6 | loop fusion | flops 6291456 | bytes 25174016 | tf_op jit(solution)/shard_map/reduce_sum | solution.py:160
  503.8 5.8 %multiply_convert_fusion = bf16[1024,2048]{1,0:T(8,128)(2,1)} fusion(f32[1024,2048]{1,0:T(8,128)} %multiply_reduce_fusion, f32[1024]{0:T(1024)S(1)} %bitcast.85), kind=kLoop, calls=%fused_computation.7 | loop fusion | flops 4194304 | bytes 12587008 | tf_op jit(solution)/shard_map/convert_element_type | solution.py:162
  509.7 37.3 %reduce-scatter.2.cloned.1.call-done = bf16[1024,256]{1,0:T(8,128)(2,1)} async-done(((bf16[1024,2048]{1,0:T(8,128)(2,1)}), bf16[1024,256]{1,0:T(8,128)(2,1)}) %reduce-scatter.2.cloned.1.call-update) | async-done | bytes 524304 | tf_op jit(solution)/shard_map/reduce_scatter | solution.py:161
  (41 shorter events, 0.4 us)
Async XLA Ops:
  6.5 53.1 %copy-start = (bf16[2048,8]{0,1:T(8,128)(2,1)S(1)}, bf16[2048,8]{0,1:T(8,128)(2,1)}, u32[]{:S(2)}) copy-start(bf16[2048,8]{0,1:T(8,128)(2,1)} %param.21) | copy-start | bytes 98308
  6.5 148.6 %all-gather.12.cloned.1.call-start = ((), (), s32[]{:S(2)}) async-start(), calls=%async_computation.5 | async-start | bytes 1114112 | tf_op jit(solution)/shard_map/all_gather | solution.py:102
  7.3 204.3 %all-gather.6.cloned.1.call-start = ((), (), s32[]{:S(2)}) async-start(), calls=%async_computation.2 | async-start | bytes 4456448 | tf_op jit(solution)/shard_map/all_gather | solution.py:127
  8.0 257.0 %all-gather.10.cloned.1.call-start = ((), (), s32[]{:S(2)}) async-start(), calls=%async_computation.4 | async-start | bytes 4456448 | tf_op jit(solution)/shard_map/all_gather | solution.py:101
  8.7 303.1 %all-gather.8.cloned.1.call-start = ((), (), s32[]{:S(2)}) async-start(), calls=%async_computation.3 | async-start | bytes 2228224 | tf_op jit(solution)/shard_map/all_gather | solution.py:90
  9.3 382.3 %all-gather.14.cloned.1.call-start = ((), (), s32[]{:S(2)}) async-start(), calls=%async_computation.6 | async-start | bytes 8912896 | tf_op jit(solution)/shard_map/all_gather | solution.py:155
  15.4 8.2 %copy-start.3 = (s32[1024,2]{0,1:T(2,128)S(1)}, s32[1024,2]{0,1:T(2,128)}, u32[]{:S(2)}) copy-start(s32[1024,2]{0,1:T(2,128)} %param.15) | copy-start | bytes 24580
  15.4 12.3 %copy-start.6 = (s32[2]{0:T(128)S(1)}, s32[2]{0:T(128)}, u32[]{:S(2)}) copy-start(s32[2]{0:T(128)} %constant.62) | copy-start | bytes 28
  15.4 12.4 %copy-start.5 = (s32[2]{0:T(128)S(1)}, s32[2]{0:T(128)}, u32[]{:S(2)}) copy-start(s32[2]{0:T(128)} %constant.65) | copy-start | bytes 28
  15.4 155.3 %all-to-all-start = ((bf16[16,128,8,256]{3,1,2,0:T(8,128)(2,1)}), bf16[16,128,8,256]{3,1,2,0:T(8,128)(2,1)}, u32[]{:S(2)}, u32[]{:S(2)}) async-start(bf16[16,128,8,256]{3,1,2,0:T(8,128)(2,1)} %stack.2), calls=%async_computation | async-start | bytes 16777216 | tf_op jit(solution)/shard_map/all_to_all | solution.py:16
  23.6 523.4 %reduce-scatter.2.cloned.1.call-start = ((), (), s32[]{:S(2)}) async-start(), calls=%async_computation.7 | async-start | bytes 4718592 | tf_op jit(solution)/shard_map/reduce_scatter | solution.py:161
  59.6 4.0 copy-start.4
  59.6 4.1 copy-start.8
  59.6 4.2 copy-start.9
  59.6 4.2 copy-start.10
  59.6 4.4 copy-start.7
  318.3 3.5 copy-start.2
  503.8 43.2 %copy-start.1 = (bf16[2048,8]{0,1:T(8,128)(2,1)S(1)}, bf16[2048,8]{0,1:T(8,128)(2,1)}, u32[]{:S(2)}) copy-start(bf16[2048,8]{0,1:T(8,128)(2,1)} %param.21) | copy-start | bytes 98308
Sparse Core Ops, SparseCore 0:
  9.5 145.5 all-gather.11
  157.2 54.2 all-gather.5
  213.7 51.2 all-gather.9
  267.0 44.8 all-gather.7
  313.8 77.7 all-gather.13
  509.8 37.1 reduce-scatter.1
